TPU v7x, 512 devices: a whole 4x4x16 slice. The times are simulated.
512 devices in a mesh: row: 16 (over y, x), adp: 32 (over z, core).
Axes of the slice: x: 4, y: 4, z: 16, core: 2. Of those that a mesh axis runs over, the one named last changes fastest.
Arguments:
- tokens: bfloat16 [8192, 8192], P('row', 'adp'), may hold values from -6 to 6
- query_base_weight: bfloat16 [8192, 8192], P(None, 'adp'), may hold values from -0.0625 to 0.0625
- adapter_down_weight: bfloat16 [32, 16, 8192], P('adp'), may hold values from -0.0625 to 0.0625
- adapter_up_weight: bfloat16 [32, 16, 8192], P('adp'), may hold values from -1.5 to 1.5
- row_adapter_index: int32 [8192, 1], P('row'), may hold values from 0 to 31; in each aligned block of 512 rows (0 to 511, 512 to 1023, ...) at most 64 rows name the same one
Outputs:
- queries: bfloat16 [8192, 8192], P('row', 'adp')
Inputs may be any that keep to these rules, and one draw needn't show every extreme that they name: `row_adapter_index`: among the 512 rows of one index of row, no adapter is used by more than 64 rows, and some adapter is used by exactly 64 rows; every adapter is used by some row.
All inputs are finite; a program needn't handle non-finite values.
Results may differ from a plain program's by a relative error of at most 0.0055.
Values may be sent and summed in bfloat16 or wider, within the bound.
No kernel may reach another device: no remote copies, remote signals or barrier semaphores. Data moves between devices by JAX's collectives and lax.ppermute only.
A program may use at most 64 MiB of HBM per device.

v0:
```python
import jax
import jax.numpy as jnp
from jax import lax
from jax.sharding import PartitionSpec as P

ADAPTER_RANK = 16
SCALE_NUMERATOR = 32


def shards(tokens, query_base_weight, adapter_down_weight, adapter_up_weight, row_adapter_index):
    row_count = tokens.shape[0]
    total_width = query_base_weight.shape[0]
    local_row_count = adapter_down_weight.shape[0]
    rank_length = adapter_down_weight.shape[1]
    groups = lax.axis_size("adp")
    total_adapters = local_row_count * groups
    capacity = 4 * row_count // total_adapters
    position = lax.axis_index("adp")
    adapter_scale = SCALE_NUMERATOR / ADAPTER_RANK
    down_weight_flat = adapter_down_weight.reshape(local_row_count * rank_length, total_width)
    shard_piece = lax.all_gather(tokens, "adp", axis=1, tiled=True)
    base_part = jnp.dot(shard_piece, query_base_weight, preferred_element_type=jnp.float32)
    down_part = lax.dot_general(
        shard_piece, down_weight_flat, (((1,), (1,)), ((), ())), preferred_element_type=jnp.float32
    )
    adapter_of = row_adapter_index[:, 0]
    every_match = adapter_of[:, None] == jnp.arange(total_adapters, dtype=jnp.int32)[None, :]
    owned_match = lax.dynamic_slice_in_dim(
        every_match, position * local_row_count, local_row_count, 1
    )
    rank_own = jnp.where(
        jnp.repeat(owned_match, rank_length, axis=1), down_part, jnp.zeros_like(down_part)
    ).astype(jnp.bfloat16)
    order_in = jnp.cumsum(every_match.astype(jnp.int32), axis=0) - 1
    slot_index = jnp.arange(capacity, dtype=jnp.int32)
    slot_table = (
        every_match.T[:, None, :] & (order_in.T[:, None, :] == slot_index[None, :, None])
    ).astype(jnp.bfloat16)
    own_table = lax.dynamic_slice_in_dim(slot_table, position * local_row_count, local_row_count, 0)
    selected_rows = jnp.einsum(
        "acn,nak->ack",
        own_table,
        rank_own.reshape(row_count, local_row_count, rank_length),
        preferred_element_type=jnp.float32,
    ).astype(jnp.bfloat16)
    update_rows = (
        jnp.einsum(
            "vbf,vfx->vbx", selected_rows, adapter_up_weight, preferred_element_type=jnp.float32
        )
        * adapter_scale
    ).astype(jnp.bfloat16)
    arrived = lax.all_to_all(
        update_rows.reshape(local_row_count * capacity, total_width),
        "adp",
        split_axis=1,
        concat_axis=0,
        tiled=True,
    )
    update = lax.dot_general(
        slot_table.reshape(total_adapters * capacity, row_count),
        arrived,
        (((0,), (0,)), ((), ())),
        preferred_element_type=jnp.float32,
    ).astype(jnp.bfloat16)
    update = lax.optimization_barrier(update)
    return (base_part + update.astype(jnp.float32)).astype(jnp.bfloat16)


def solution(mesh):
    return jax.shard_map(
        shards,
        mesh=mesh,
        in_specs=(
            P("row", "adp"),
            P(None, "adp"),
            P("adp", None, None),
            P("adp", None, None),
            P("row", None),
        ),
        out_specs=P("row", "adp"),
        check_vma=False,
    )
```

profile of v0, /device:TPU:1, one launch (start us, length us, event | category | flops | bytes accessed | tf_op | source)
XLA Modules:
  0.0 193.7 jit_solution(11247434372727005446)
XLA Ops:
  6.5 0.0 copy-start
  6.5 0.0 all-gather.2.cloned.1.call-start
  6.5 0.7 all-gather.2.cloned.1.call-update
  7.3 0.7 fusion.15
  8.0 1.2 reduce-window.6
  9.1 0.2 slice_reduce_fusion
  9.4 0.7 compare_reduce_fusion
  10.1 0.7 iota_compare_fusion.2
  10.8 0.1 copy_bitcast_fusion.1
  10.9 0.9 fusion.1
  11.8 98.9 %all-gather.2.cloned.1.call-done = bf16[512,8192]{1,0:T(8,128)(2,1)} async-done(((bf16[512,256]{1,0:T(8,128)(2,1)}), bf16[512,8192]{1,0:T(8,128)(2,1)}) %all-gather.2.cloned.1.call-update) | async-done | bytes 8388624 | tf_op jit(solution)/shard_map/all_gather | solution.py:21
  110.7 5.8 %fusion.6 = bf16[64,16]{1,0:T(8,128)(2,1)S(1)} fusion(bf16[512,8192]{1,0:T(8,128)(2,1)} %all-gather.2.cloned.1.call-done, bf16[1,16,8192]{2,1,0:T(8,128)(2,1)} %param.7, pred[512]{0:T(512)(128)(4,1)S(1)} %compare_reduce_fusion, pred[32,64,512]{2,1,0:T(32,128)(4,1)S(1)} %fusion.1, s32[]{:T(128)S(6)} %select_n.8), kind=kOutput, calls=%fused_computation.11 | convolution fusion | flops 135283712 | bytes 8686084 | tf_op jit(solution)/shard_map/acn,nak->ack/dot_general | solution.py:40
  116.5 0.0 copy-done
  116.5 0.4 fusion
  117.0 0.0 slice-start
  117.0 0.1 copy.13
  117.1 63.3 %all_to_all.16 = bf16[64,32,256]{2,0,1:T(8,128)(2,1)S(1)} all-to-all(bf16[64,32,256]{2,0,1:T(8,128)(2,1)S(1)} %bitcast.33), channel_id=1, replica_groups=mesh['row'=16,'adp'=32] {'adp'}, dimensions={1} | all-to-all | bytes 2097152 | tf_op jit(solution)/shard_map/all_to_all | solution.py:52
  180.4 0.0 slice-start.1
  180.4 0.0 copy-start.1
  180.4 1.3 fusion.3
  181.7 0.0 slice-done
  181.7 0.9 slice-done.1
  182.6 1.3 copy-done.1
  183.8 3.0 %fusion.2 = bf16[512,256]{1,0:T(8,128)(2,1)} fusion(bf16[512,8192]{1,0:T(8,128)(2,1)S(1)} %bitcast.38, bf16[8192,256]{1,0:T(8,128)(2,1)S(1)} %copy-done.1, bf16[512,256]{1,0:T(8,128)(2,1)S(1)} %fusion.3), kind=kOutput, calls=%fused_computation.6 | convolution fusion | flops 2147876864 | bytes 13107200 | tf_op jit(solution)/shard_map/dot_general | solution.py:22
  (3 shorter events, 0.0 us)
Async XLA Ops:
  6.5 110.0 %copy-start = (bf16[1,16,8192]{2,1,0:T(8,128)(2,1)S(1)}, bf16[1,16,8192]{2,1,0:T(8,128)(2,1)}, u32[]{:S(2)}) copy-start(bf16[1,16,8192]{2,1,0:T(8,128)(2,1)} %param.8) | copy-start | bytes 786436
  6.5 104.2 %all-gather.2.cloned.1.call-start = ((), (), s32[]{:S(2)}) async-start(), calls=%async_computation.1 | async-start | bytes 8650752 | tf_op jit(solution)/shard_map/all_gather | solution.py:21
  117.0 64.7 %slice-start = ((s8[8388608]{0:T(1024)(128)(4,1)}), s8[4194304]{0:T(1024)(128)(4,1)S(1)}, s32[]{:S(2)}) async-start(s8[8388608]{0:T(1024)(128)(4,1)} %bitcast.37), calls=%async_computation.2 | async-start | bytes 8388608
  180.4 2.2 %slice-start.1 = ((s8[8388608]{0:T(1024)(128)(4,1)}), s8[4194304]{0:T(1024)(128)(4,1)S(1)}, s32[]{:S(2)}) async-start(s8[8388608]{0:T(1024)(128)(4,1)} %bitcast.37), calls=%async_computation.3 | async-start | bytes 8388608
  180.4 3.5 %copy-start.1 = (bf16[8192,256]{1,0:T(8,128)(2,1)S(1)}, bf16[8192,256]{1,0:T(8,128)(2,1)}, u32[]{:S(2)}) copy-start(bf16[8192,256]{1,0:T(8,128)(2,1)} %param.6) | copy-start | bytes 12582916
Sparse Core Ops, SparseCore 0:
  9.4 101.2 all-gather.1
where the time goes:
time: 194 us
  waiting for transfers between devices  99.6 us (51%)
  blocking collectives  63.3 us (33%)
  between operations  13.5 us (7%)
  matrix products  10.6 us (5%)
  other arithmetic  4.29 us (2%)
  local copies, waits for them, and re-layouts  2.49 us (1%)
    all_gather x1, waiting for transfers between devices, shards(): shard_piece = lax.all_gather(tokens, 'adp', axis=1, tiled=True)  98.9 us
    all_to_all x1, blocking collectives, shards(): lax.all_to_all(update_rows.reshape(local_row_count * capacity, total_widt...  63.3 us
    dot_general x1, matrix products, shards(): jnp.einsum('acn,nak->ack', own_table, rank_own.reshape(row_count, local_r...  5.83 us
  transfers between devices with their start and end apart: 1, of which 1 were waited for; matrix products, arithmetic and copies ran while one was open for 2% of the time, Pallas kernels for 0%

commit v1 on v0

v1 whole, which is shorter than its diff:
```python
import jax
import jax.numpy as jnp
from jax import lax
from jax.experimental import pallas as pl
from jax.experimental.pallas import tpu as pltpu
from jax.sharding import PartitionSpec as P

ADAPTER_RANK = 16
SCALE_NUMERATOR = 32


def _sum_kernel(x_ref, w_ref, o_ref):
    part = jnp.dot(x_ref[0], w_ref[0], preferred_element_type=jnp.float32)

    @pl.when(pl.program_id(0) == 0)
    def _():
        o_ref[...] = part

    @pl.when(pl.program_id(0) > 0)
    def _():
        o_ref[...] += part


def _block_sum(x, w):
    steps, rows, width = x.shape
    cols = w.shape[2]
    return pl.pallas_call(
        _sum_kernel,
        grid=(steps,),
        in_specs=[
            pl.BlockSpec((1, rows, width), lambda i: (i, 0, 0)),
            pl.BlockSpec((1, width, cols), lambda i: (i, 0, 0)),
        ],
        out_specs=pl.BlockSpec((rows, cols), lambda i: (0, 0)),
        out_shape=jax.ShapeDtypeStruct((rows, cols), jnp.float32),
        cost_estimate=pl.CostEstimate(
            flops=2 * steps * rows * width * cols,
            bytes_accessed=2 * steps * width * (rows + cols) + 4 * rows * cols,
            transcendentals=0,
        ),
    )(x, w)


def shards(tokens, query_base_weight, adapter_down_weight, adapter_up_weight, row_adapter_index):
    rows, width = tokens.shape
    total_width, cols = query_base_weight.shape
    groups = lax.axis_size("adp")
    chips = groups // 2
    rank = adapter_down_weight.shape[1]
    adapters = groups
    core = lax.axis_index("adp") % 2
    row = lax.axis_index("row")
    scale = SCALE_NUMERATOR / ADAPTER_RANK
    same_core = [[2 * z + c for z in range(chips)] for c in range(2)]
    swap = [(a, a ^ 1) for a in range(groups)]

    gathered = lax.all_gather(tokens, "adp", axis=0, tiled=False, axis_index_groups=same_core)

    by_core = query_base_weight.reshape(chips, 2, width, cols)
    mine = lax.dynamic_slice_in_dim(by_core, core, 1, 1)[:, 0]
    theirs = lax.dynamic_slice_in_dim(by_core, 1 - core, 1, 1)[:, 0]
    partner = lax.ppermute(theirs, "adp", swap)

    tables = jnp.concatenate(
        [
            lax.dynamic_slice_in_dim(adapter_down_weight[0], row, 1, 0),
            lax.dynamic_slice_in_dim(adapter_up_weight[0], row, 1, 0),
        ],
        axis=0,
    )
    pieces = tables.reshape(2, groups, width).transpose(1, 0, 2)
    pieces = lax.all_to_all(pieces, "adp", split_axis=0, concat_axis=0, tiled=True)
    pieces = lax.all_gather(pieces, "row", axis=0, tiled=False)
    down = pieces[:, :, 0, :].reshape(rank * adapters, width)
    up = pieces[:, :, 1, :].reshape(rank * adapters, cols)

    chosen = (
        row_adapter_index[:, 0][None, :] == jnp.arange(adapters, dtype=jnp.int32)[:, None]
    )
    sums = lax.dot_general(
        down, tokens, (((1,), (1,)), ((), ())), preferred_element_type=jnp.float32
    ).reshape(rank, adapters, rows)
    sums = jnp.where(chosen[None], sums, 0.0).sum(axis=1)
    sums = sums + lax.ppermute(sums, "adp", swap)
    sums = lax.all_gather(sums, "adp", axis=0, tiled=False, axis_index_groups=same_core)
    ranks = sums.sum(axis=0).astype(jnp.bfloat16)
    spread = jnp.where(chosen[None], ranks[:, None, :], jnp.zeros((), jnp.bfloat16))
    update = (
        lax.dot_general(
            spread.reshape(rank * adapters, rows),
            up,
            (((0,), (0,)), ((), ())),
            preferred_element_type=jnp.float32,
        )
        * scale
    ).astype(jnp.bfloat16)

    other = _block_sum(gathered, partner)
    other = lax.ppermute(other, "adp", swap)
    own = _block_sum(gathered, mine)
    return (own + other + update.astype(jnp.float32)).astype(jnp.bfloat16)


def solution(mesh):
    return jax.shard_map(
        shards,
        mesh=mesh,
        in_specs=(
            P("row", "adp"),
            P(None, "adp"),
            P("adp", None, None),
            P("adp", None, None),
            P("row", None),
        ),
        out_specs=P("row", "adp"),
        check_vma=False,
    )
```

time: 194 us -> 139 us (0.72)
  waiting for transfers between devices: 99.6 us -> 13.7 us
  starting transfers between devices: 0.01 us -> 32.3 us
  Pallas kernels: 0 us -> 22.8 us
  blocking collectives: 63.3 us -> 47.6 us
  matrix products: 10.6 us -> 0.68 us
  local copies, waits for them, and re-layouts: 2.49 us -> 5.09 us
    all_gather x1, waiting for transfers between devices: 98.9 us -> 0.02 us  [shards(): lax.all_gather(tokens, 'adp', axis=0, tiled=False, axis_index_groups=same...]
    all_to_all x1 -> x0, blocking collectives: 63.3 us -> none  [shards(): lax.all_to_all(update_rows.reshape(local_row_count * capacity, total_widt...]
    all_gather x0 -> x2, blocking collectives: none -> 47.6 us  [the longest x1 26.8 us: shards(): lax.all_gather(sums, 'adp', axis=0, tiled=False, axis_index_groups=same_c...]
    pallas_call x0 -> x2, Pallas kernels: none -> 22.8 us  [_block_sum(): pl.pallas_call(_sum_kernel, grid=(steps,), in_specs=[pl.BlockSpec((1, row...]
    ppermute x0 -> x3, starting transfers between devices: none -> 22.3 us  [the longest x1 8.74 us: shards(): partner = lax.ppermute(theirs, 'adp', swap)]
    all_to_all x0 -> x1, waiting for transfers between devices: none -> 12.1 us  [shards(): lax.all_to_all(pieces, 'adp', split_axis=0, concat_axis=0, tiled=True)]
    all_to_all x0 -> x1, starting transfers between devices: none -> 10 us  [shards(): lax.all_to_all(pieces, 'adp', split_axis=0, concat_axis=0, tiled=True)]
    dot_general x4 -> x2, matrix products: 10.6 us -> 0.68 us  [the longest x1 0.34 us: shards(): lax.dot_general(spread.reshape(rank * adapters, rows), up, (((0,), (0,)),...]
  transfers between devices with their start and end apart: 1 -> 5, of which waited for: 1 -> 2; matrix products, arithmetic and copies ran while one was open for 2% -> 5% of each run, Pallas kernels for 0% -> 8%
where the time goes in v1:
time: 139 us; the launch traced here: 138 us
  blocking collectives  47.6 us (34%)
  starting transfers between devices  32.3 us (23%)
  Pallas kernels  22.8 us (16%)
  waiting for transfers between devices  13.7 us (10%)
  between operations  13.5 us (10%)
  local copies, waits for them, and re-layouts  5.09 us (4%)
  other arithmetic  2.62 us (2%)
    all_gather x1, blocking collectives, shards(): lax.all_gather(sums, 'adp', axis=0, tiled=False, axis_index_groups=same_c...  26.8 us
    pallas_call x2, Pallas kernels, _block_sum(): pl.pallas_call(_sum_kernel, grid=(steps,), in_specs=[pl.BlockSpec((1, row...  22.8 us
    all_gather x1, blocking collectives, shards(): pieces = lax.all_gather(pieces, 'row', axis=0, tiled=False)  20.9 us
    all_to_all x1, waiting for transfers between devices, shards(): lax.all_to_all(pieces, 'adp', split_axis=0, concat_axis=0, tiled=True)  12.1 us
    all_to_all x1, starting transfers between devices, shards(): lax.all_to_all(pieces, 'adp', split_axis=0, concat_axis=0, tiled=True)  10 us
    ppermute x1, starting transfers between devices, shards(): partner = lax.ppermute(theirs, 'adp', swap)  8.74 us
    ppermute x1, starting transfers between devices, shards(): sums = sums + lax.ppermute(sums, 'adp', swap)  7.09 us
    ppermute x1, starting transfers between devices, shards(): other = lax.ppermute(other, 'adp', swap)  6.51 us
  transfers between devices with their start and end apart: 5, of which 2 were waited for; matrix products, arithmetic and copies ran while one was open for 5% of the time, Pallas kernels for 8%

profile of v1, /device:TPU:1, one launch (start us, length us, event | category | flops | bytes accessed | tf_op | source)
XLA Modules:
  0.0 138.4 jit_solution(17892581331565860809)
XLA Ops:
  6.5 0.0 all-gather.5.cloned.1.call-start
  6.5 0.7 all-gather.5.cloned.1.call-update
  7.3 0.0 copy-start.1
  7.3 0.0 copy-start
  7.3 4.0 %dynamic-slice_bitcast_fusion = (bf16[16,256,256]{2,1,0:T(8,128)(2,1)S(1)}, bf16[16,256,256]{2,1,0:T(8,128)(2,1)}) fusion(bf16[16,2,256,256]{3,2,1,0:T(8,128)(2,1)} %bitcast.29, s32[]{:T(128)S(6)} %select_n.37, s32[]{:T(128)S(6)} %select_n.36), kind=kLoop, calls=%fused_computation | loop fusion | bytes 8388616 | tf_op jit(solution)/shard_map/squeeze | solution.py:61
  11.2 8.7 %collective-permute-start = (bf16[16,256,256]{2,1,0:T(8,128)(2,1)S(1)}, bf16[16,256,256]{2,1,0:T(8,128)(2,1)}, u32[]{:S(2)}, u32[]{:S(2)}) collective-permute-start(bf16[16,256,256]{2,1,0:T(8,128)(2,1)S(1)} %get-tuple-element.5), channel_id=1, source_target_pairs={{0,1},{1,0},{2,3},{3,2},{4,5},{5,4},{6,7},{7,6},{8,9},{9,8},{10,11... | collective-permute-start | bytes 6291464 | tf_op jit(solution)/shard_map/ppermute | solution.py:62
  20.0 1.0 constant_dynamic-slice_fusion
  21.0 0.7 maximum_bitcast_fusion
  21.7 10.0 %all-to-all-start = ((bf16[32,2,256]{2,1,0:T(2,128)(2,1)}), bf16[32,2,256]{2,1,0:T(2,128)(2,1)S(1)}, u32[]{:S(2)}, u32[]{:S(2)}) async-start(bf16[32,2,256]{2,1,0:T(2,128)(2,1)} %maximum_bitcast_fusion), calls=%async_computation | async-start | bytes 65536 | tf_op jit(solution)/shard_map/all_to_all | solution.py:72
  31.8 12.1 %all-to-all-done = bf16[32,2,256]{2,1,0:T(2,128)(2,1)S(1)} async-done(((bf16[32,2,256]{2,1,0:T(2,128)(2,1)}), bf16[32,2,256]{2,1,0:T(2,128)(2,1)S(1)}, u32[]{:S(2)}, u32[]{:S(2)}) %all-to-all-start) | async-done | bytes 32800 | tf_op jit(solution)/shard_map/all_to_all | solution.py:72
  43.9 20.9 %all-gather.1 = bf16[512,2,256]{2,1,0:T(2,128)(2,1)S(1)} all-gather(bf16[32,2,256]{2,1,0:T(2,128)(2,1)S(1)} %all-to-all-done), channel_id=3, replica_groups=mesh['row'=16,'adp'=32] {'row'}, dimensions={0}, use_global_device_ids=true | all-gather | bytes 557056 | tf_op jit(solution)/shard_map/all_gather | solution.py:73
  64.8 0.1 copy.16
  64.9 0.3 fusion
  65.2 7.1 %collective-permute-start.2 = (f32[16,512]{1,0:T(8,128)S(1)}, f32[16,512]{1,0:T(8,128)S(1)}, u32[]{:S(2)}, u32[]{:S(2)}) collective-permute-start(f32[16,512]{1,0:T(8,128)S(1)} %fusion), channel_id=1, source_target_pairs={{0,1},{1,0},{2,3},{3,2},{4,5},{5,4},{6,7},{7,6},{8,9},{9,8},{10,11... | collective-permute-start | bytes 98312 | tf_op jit(solution)/shard_map/ppermute | solution.py:84
  72.3 0.8 collective-permute-done.2
  73.2 26.8 %all-gather.2 = f32[256,512]{1,0:T(8,128)S(1)} all-gather(f32[16,512]{1,0:T(8,128)S(1)} %add.29), channel_id=4, replica_groups={{0,2,4,6,8,10,12,14,16,18,20,22,24,26,28,30},{1,3,5,7,9,11,13,15,17,19,..., dimensions={0}, use_global_device_ids=true | all-gather | bytes 557056 | tf_op jit(solution)/shard_map/all_gather | solution.py:85
  100.0 0.0 collective-permute-done.w_ref
  100.0 0.0 all-gather.5.cloned.1.call-done
  100.0 11.4 %shard_map.56 = f32[512,256]{1,0:T(8,128)} custom-call(bf16[16,512,256]{2,1,0:T(8,128)(2,1)} %bitcast.27, bf16[16,256,256]{2,1,0:T(8,128)(2,1)} %collective-permute-done.w_ref), custom_call_target="tpu_custom_call" | custom-call | flops 1073741824 | bytes 6815744 | tf_op jit(solution)/shard_map/pallas_call | solution.py:27
  111.4 6.5 %collective-permute-start.1 = (f32[512,256]{1,0:T(8,128)}, f32[512,256]{1,0:T(8,128)S(1)}, u32[]{:S(2)}, u32[]{:S(2)}) collective-permute-start(f32[512,256]{1,0:T(8,128)} %shard_map.56), channel_id=1, source_target_pairs={{0,1},{1,0},{2,3},{3,2},{4,5},{5,4},{6,7},{7,6},{8,9},{9,8},{10,11... | collective-permute-start | bytes 1572872 | tf_op jit(solution)/shard_map/ppermute | solution.py:99
  118.0 0.3 fusion.2
  118.3 11.4 %shard_map.55 = f32[512,256]{1,0:T(8,128)} custom-call(bf16[16,512,256]{2,1,0:T(8,128)(2,1)} %bitcast.28, bf16[16,256,256]{2,1,0:T(8,128)(2,1)} %get-tuple-element.6.w_ref), custom_call_target="tpu_custom_call" | custom-call | flops 1073741824 | bytes 6815744 | tf_op jit(solution)/shard_map/pallas_call | solution.py:27
  129.7 0.0 collective-permute-done.1
  129.7 1.8 %add_convert_fusion = bf16[512,256]{1,0:T(8,128)(2,1)} fusion(f32[512,256]{1,0:T(8,128)S(1)} %fusion.2, f32[512,256]{1,0:T(8,128)} %shard_map.55, f32[512,256]{1,0:T(8,128)S(1)} %collective-permute-done.1), kind=kLoop, calls=%fused_computation.7 | loop fusion | flops 393216 | bytes 1835008 | tf_op jit(solution)/shard_map/convert_element_type | solution.py:101
  (7 shorter events, 0.1 us)
Async XLA Ops:
  6.5 93.5 %all-gather.5.cloned.1.call-start = ((), (), s32[]{:S(2)}) async-start(), calls=%async_computation.1 | async-start | bytes 4456448 | tf_op jit(solution)/shard_map/all_gather | solution.py:57
  7.3 24.5 %copy-start.1 = (s32[512,1]{0,1:T(1,128)S(1)}, s32[512,1]{0,1:T(1,128)}, u32[]{:S(2)}) copy-start(s32[512,1]{0,1:T(1,128)} %param.9) | copy-start | bytes 6148
  7.3 57.6 %copy-start = (bf16[512,256]{1,0:T(8,128)(2,1)S(1)}, bf16[512,256]{1,0:T(8,128)(2,1)}, u32[]{:S(2)}) copy-start(bf16[512,256]{1,0:T(8,128)(2,1)} %param.5) | copy-start | bytes 786436
  11.2 88.7 %collective-permute-start = (bf16[16,256,256]{2,1,0:T(8,128)(2,1)S(1)}, bf16[16,256,256]{2,1,0:T(8,128)(2,1)}, u32[]{:S(2)}, u32[]{:S(2)}) collective-permute-start(bf16[16,256,256]{2,1,0:T(8,128)(2,1)S(1)} %get-tuple-element.5), channel_id=1, source_target_pairs={{0,1},{1,0},{2,3},{3,2},{4,5},{5,4},{6,7},{7,6},{8,9},{9,8},{10,11... | collective-permute-start | bytes 6291464 | tf_op jit(solution)/shard_map/ppermute | solution.py:62
  21.7 22.2 %all-to-all-start = ((bf16[32,2,256]{2,1,0:T(2,128)(2,1)}), bf16[32,2,256]{2,1,0:T(2,128)(2,1)S(1)}, u32[]{:S(2)}, u32[]{:S(2)}) async-start(bf16[32,2,256]{2,1,0:T(2,128)(2,1)} %maximum_bitcast_fusion), calls=%async_computation | async-start | bytes 65536 | tf_op jit(solution)/shard_map/all_to_all | solution.py:72
  65.2 7.9 %collective-permute-start.2 = (f32[16,512]{1,0:T(8,128)S(1)}, f32[16,512]{1,0:T(8,128)S(1)}, u32[]{:S(2)}, u32[]{:S(2)}) collective-permute-start(f32[16,512]{1,0:T(8,128)S(1)} %fusion), channel_id=1, source_target_pairs={{0,1},{1,0},{2,3},{3,2},{4,5},{5,4},{6,7},{7,6},{8,9},{9,8},{10,11... | collective-permute-start | bytes 98312 | tf_op jit(solution)/shard_map/ppermute | solution.py:84
  111.4 18.3 %collective-permute-start.1 = (f32[512,256]{1,0:T(8,128)}, f32[512,256]{1,0:T(8,128)S(1)}, u32[]{:S(2)}, u32[]{:S(2)}) collective-permute-start(f32[512,256]{1,0:T(8,128)} %shard_map.56), channel_id=1, source_target_pairs={{0,1},{1,0},{2,3},{3,2},{4,5},{5,4},{6,7},{7,6},{8,9},{9,8},{10,11... | collective-permute-start | bytes 1572872 | tf_op jit(solution)/shard_map/ppermute | solution.py:99
Sparse Core Ops, SparseCore 0:
  9.4 76.9 all-gather.4

commit v2 on v1

v2 whole, which is shorter than its diff:
```python
import jax
import jax.numpy as jnp
from jax import lax
from jax.experimental import pallas as pl
from jax.experimental.pallas import tpu as pltpu
from jax.experimental.layout import Layout, with_layout_constraint
from jax.sharding import PartitionSpec as P

ADAPTER_RANK = 16
SCALE_NUMERATOR = 32


def _block_sum(x, w):
    return lax.dot_general(
        x, w, (((0, 2), (0, 1)), ((), ())), preferred_element_type=jnp.float32
    )


def shards(tokens, query_base_weight, adapter_down_weight, adapter_up_weight, row_adapter_index):
    rows, width = tokens.shape
    total_width, cols = query_base_weight.shape
    groups = lax.axis_size("adp")
    chips = groups // 2
    rank = adapter_down_weight.shape[1]
    adapters = groups
    core = lax.axis_index("adp") % 2
    row = lax.axis_index("row")
    scale = SCALE_NUMERATOR / ADAPTER_RANK
    same_core = [[2 * z + c for z in range(chips)] for c in range(2)]
    swap = [(a, a ^ 1) for a in range(groups)]

    gathered = lax.all_gather(tokens, "adp", axis=0, tiled=False, axis_index_groups=same_core)

    near = 4
    share = rank // near
    first = (row % near) * share
    pieces = jnp.stack(
        [
            lax.dynamic_slice_in_dim(adapter_down_weight[0], first, share, 0),
            lax.dynamic_slice_in_dim(adapter_up_weight[0], first, share, 0),
        ]
    )
    pieces = pieces.reshape(2 * share, groups, width).transpose(1, 0, 2)
    pieces, query_base_weight = lax.optimization_barrier((pieces, query_base_weight))
    pieces = lax.all_to_all(pieces, "adp", split_axis=0, concat_axis=0, tiled=True)
    pieces = pieces.reshape(adapters, 2, share, width).transpose(1, 2, 0, 3)
    lines = [[near * y + x for x in range(near)] for y in range(lax.axis_size("row") // near)]
    pieces = lax.all_gather(pieces, "row", axis=0, tiled=False, axis_index_groups=lines)
    down = pieces[:, 0].reshape(rank * adapters, width)
    up = pieces[:, 1].reshape(rank * adapters, cols)

    by_core = query_base_weight.reshape(chips, 2, width, cols)
    theirs = lax.dynamic_slice_in_dim(by_core, 1 - core, 1, 1)[:, 0]
    theirs = with_layout_constraint(theirs, Layout(major_to_minor=(0, 1, 2)))
    partner = lax.ppermute(theirs, "adp", swap)
    partner = with_layout_constraint(partner, Layout(major_to_minor=(0, 1, 2)))

    chosen = (
        row_adapter_index[:, 0][None, :] == jnp.arange(adapters, dtype=jnp.int32)[:, None]
    )
    sums = lax.dot_general(
        down, tokens, (((1,), (1,)), ((), ())), preferred_element_type=jnp.float32
    ).reshape(rank, adapters, rows)
    sums = jnp.where(chosen[None], sums, 0.0).sum(axis=1)
    sums = sums + lax.ppermute(sums, "adp", swap)
    sums = lax.all_gather(sums, "adp", axis=0, tiled=False, axis_index_groups=same_core)
    ranks = sums.sum(axis=0).astype(jnp.bfloat16)
    spread = jnp.where(chosen[None], ranks[:, None, :], jnp.zeros((), jnp.bfloat16))
    update = (
        lax.dot_general(
            spread.reshape(rank * adapters, rows),
            up,
            (((0,), (0,)), ((), ())),
            preferred_element_type=jnp.float32,
        )
        * scale
    ).astype(jnp.bfloat16)
    update = lax.optimization_barrier(update)

    other = _block_sum(gathered, partner)
    other = lax.ppermute(other, "adp", swap)
    own = _block_sum(gathered, lax.dynamic_slice_in_dim(by_core, core, 1, 1)[:, 0])
    return (own + other + update.astype(jnp.float32)).astype(jnp.bfloat16)


def solution(mesh):
    return jax.shard_map(
        shards,
        mesh=mesh,
        in_specs=(
            P("row", "adp"),
            P(None, "adp"),
            P("adp", None, None),
            P("adp", None, None),
            P("row", None),
        ),
        out_specs=P("row", "adp"),
        check_vma=False,
    )
```

time: 139 us -> 117 us (0.84)
  Pallas kernels: 22.8 us -> 0 us
  blocking collectives: 47.6 us -> 41.7 us
  matrix products: 0.68 us -> 6.25 us
  waiting for transfers between devices: 13.7 us -> 18.4 us
  other arithmetic: 2.62 us -> 0.34 us
    pallas_call x2 -> x0, Pallas kernels: 22.8 us -> none  [_block_sum(): pl.pallas_call(_sum_kernel, grid=(steps,), in_specs=[pl.BlockSpec((1, row...]
    all_gather x1, blocking collectives: 20.9 us -> 11.8 us  [shards(): lax.all_gather(pieces, 'row', axis=0, tiled=False, axis_index_groups=lines)]
    dot_general x0 -> x2, matrix products: none -> 5.56 us  [_block_sum(): lax.dot_general(x, w, (((0, 2), (0, 1)), ((), ())), preferred_element_typ...]
    all_to_all x1, waiting for transfers between devices: 12.1 us -> 16.8 us  [shards(): lax.all_to_all(pieces, 'adp', split_axis=0, concat_axis=0, tiled=True)]
    all_gather x1, blocking collectives: 26.8 us -> 29.9 us  [shards(): lax.all_gather(sums, 'adp', axis=0, tiled=False, axis_index_groups=same_c...]
    squeeze x1, local copies, waits for them, and re-layouts: 3.95 us -> 1.74 us  [shards(): theirs = lax.dynamic_slice_in_dim(by_core, 1 - core, 1, 1)[:, 0]]
    ppermute x1, starting transfers between devices: 7.09 us -> 5.24 us  [shards(): sums = sums + lax.ppermute(sums, 'adp', swap)]
    convert_element_type x1, other arithmetic: 1.82 us -> 0.15 us  [shards(): return (own + other + update.astype(jnp.float32)).astype(jnp.bfloat16)]
  transfers between devices with their start and end apart: 5 -> 5, of which waited for: 2 -> 2; matrix products, arithmetic and copies ran while one was open for 5% -> 5% of each run, Pallas kernels for 8% -> 0%
where the time goes in v2:
time: 117 us; the launch traced here: 116 us
  blocking collectives  41.7 us (36%)
  starting transfers between devices  31.4 us (27%)
  waiting for transfers between devices  18.4 us (16%)
  between operations  13.6 us (12%)
  matrix products  6.25 us (5%)
  local copies, waits for them, and re-layouts  4.5 us (4%)
    all_gather x1, blocking collectives, shards(): lax.all_gather(sums, 'adp', axis=0, tiled=False, axis_index_groups=same_c...  29.9 us
    all_to_all x1, waiting for transfers between devices, shards(): lax.all_to_all(pieces, 'adp', split_axis=0, concat_axis=0, tiled=True)  16.8 us
    all_gather x1, blocking collectives, shards(): lax.all_gather(pieces, 'row', axis=0, tiled=False, axis_index_groups=lines)  11.8 us
    all_to_all x1, starting transfers between devices, shards(): lax.all_to_all(pieces, 'adp', split_axis=0, concat_axis=0, tiled=True)  10 us
    ppermute x1, starting transfers between devices, shards(): partner = lax.ppermute(theirs, 'adp', swap)  8.75 us
    ppermute x1, starting transfers between devices, shards(): other = lax.ppermute(other, 'adp', swap)  7.4 us
    dot_general x2, matrix products, _block_sum(): lax.dot_general(x, w, (((0, 2), (0, 1)), ((), ())), preferred_element_typ...  5.56 us
    ppermute x1, starting transfers between devices, shards(): sums = sums + lax.ppermute(sums, 'adp', swap)  5.24 us
  transfers between devices with their start and end apart: 5, of which 2 were waited for; matrix products, arithmetic and copies ran while one was open for 5% of the time, Pallas kernels for 0%

profile of v2, /device:TPU:1, one launch (start us, length us, event | category | flops | bytes accessed | tf_op | source)
XLA Modules:
  0.0 116.2 jit_solution(6262111773142520264)
XLA Ops:
  6.5 0.7 all-gather.5.cloned.1.call-update
  7.3 1.0 constant_dynamic-slice_fusion
  8.3 0.1 pad_maximum_fusion
  8.4 0.1 reshape.56
  8.5 1.7 %dynamic-slice_bitcast_fusion = bf16[16,256,256]{2,1,0:T(8,128)(2,1)S(1)} fusion(bf16[16,2,256,256]{3,2,1,0:T(8,128)(2,1)} %bitcast.41, s32[]{:T(128)S(6)} %select_n.43), kind=kLoop, calls=%fused_computation.2 | loop fusion | bytes 4194308 | tf_op jit(solution)/shard_map/squeeze | solution.py:53
  10.3 8.7 %collective-permute-start = (bf16[16,256,256]{2,1,0:T(8,128)(2,1)S(1)}, bf16[16,256,256]{2,1,0:T(8,128)(2,1)}, u32[]{:S(2)}, u32[]{:S(2)}) collective-permute-start(bf16[16,256,256]{2,1,0:T(8,128)(2,1)S(1)} %dynamic-slice_bitcast_fusion), channel_id=1, source_target_pairs={{0,1},{1,0},{2,3},{3,2},{4,5},{5,4},{6,7},{7,6},{8,9},{9,8},{10,11... | collective-permute-start | bytes 6291464 | tf_op jit(solution)/shard_map/ppermute | solution.py:55
  19.0 0.7 copy.27
  19.7 10.0 %all-to-all-start = ((bf16[32,8,256]{2,1,0:T(8,128)(2,1)}), bf16[32,8,256]{2,1,0:T(8,128)(2,1)S(1)}, u32[]{:S(2)}, u32[]{:S(2)}) async-start(bf16[32,8,256]{2,1,0:T(8,128)(2,1)} %copy.27), calls=%async_computation | async-start | bytes 262144 | tf_op jit(solution)/shard_map/all_to_all | solution.py:45
  29.8 16.8 %all-to-all-done = bf16[32,8,256]{2,1,0:T(8,128)(2,1)S(1)} async-done(((bf16[32,8,256]{2,1,0:T(8,128)(2,1)}), bf16[32,8,256]{2,1,0:T(8,128)(2,1)S(1)}, u32[]{:S(2)}, u32[]{:S(2)}) %all-to-all-start) | async-done | bytes 131104 | tf_op jit(solution)/shard_map/all_to_all | solution.py:45
  46.6 11.8 %all-gather.1 = bf16[8,4,32,256]{3,2,1,0:T(8,128)(2,1)S(1)} all-gather(bf16[2,4,32,256]{3,2,1,0:T(8,128)(2,1)S(1)} %bitcast.43), channel_id=3, replica_groups={{0,32,64,96},{128,160,192,224},{256,288,320,352},{384,416,448,480},{1,3..., dimensions={0}, use_global_device_ids=true | all-gather | bytes 655360 | tf_op jit(solution)/shard_map/all_gather | solution.py:48
  58.5 0.3 fusion.3
  58.8 5.2 %collective-permute-start.2 = (f32[16,512]{1,0:T(8,128)S(1)}, f32[16,512]{1,0:T(8,128)S(1)}, u32[]{:S(2)}, u32[]{:S(2)}) collective-permute-start(f32[16,512]{1,0:T(8,128)S(1)} %fusion.3), channel_id=1, source_target_pairs={{0,1},{1,0},{2,3},{3,2},{4,5},{5,4},{6,7},{7,6},{8,9},{9,8},{10,11... | collective-permute-start | bytes 98312 | tf_op jit(solution)/shard_map/ppermute | solution.py:65
  64.1 0.8 collective-permute-done.2
  64.9 29.9 %all-gather.2 = f32[256,512]{1,0:T(8,128)S(1)} all-gather(f32[16,512]{1,0:T(8,128)S(1)} %add.33), channel_id=4, replica_groups={{0,2,4,6,8,10,12,14,16,18,20,22,24,26,28,30},{1,3,5,7,9,11,13,15,17,19,..., dimensions={0}, use_global_device_ids=true | all-gather | bytes 557056 | tf_op jit(solution)/shard_map/all_gather | solution.py:66
  94.9 0.0 collective-permute-done
  95.0 0.0 all-gather.5.cloned.1.call-done
  95.0 0.0 copy-start
  95.0 4.3 %convolution_bitcast_fusion = f32[512,256]{0,1:T(8,128)S(1)} fusion(bf16[16,256,256]{2,1,0:T(8,128)(2,1)} %collective-permute-done, bf16[16,512,256]{2,1,0:T(8,128)(2,1)} %bitcast.49), kind=kOutput, calls=%fused_computation.7 | convolution fusion | flops 1073741824 | bytes 6815744 | tf_op jit(solution)/shard_map/dot_general | solution.py:14
  99.3 7.4 %collective-permute-start.1 = (f32[512,256]{0,1:T(8,128)S(1)}, f32[512,256]{0,1:T(8,128)S(1)}, u32[]{:S(2)}, u32[]{:S(2)}) collective-permute-start(f32[512,256]{0,1:T(8,128)S(1)} %convolution_bitcast_fusion), channel_id=1, source_target_pairs={{0,1},{1,0},{2,3},{3,2},{4,5},{5,4},{6,7},{7,6},{8,9},{9,8},{10,11... | collective-permute-start | bytes 1572872 | tf_op jit(solution)/shard_map/ppermute | solution.py:81
  106.7 0.3 fusion.7
  107.1 1.3 %fusion.4 = f32[512,256]{0,1:T(8,128)S(1)} fusion(bf16[16,512,256]{2,1,0:T(8,128)(2,1)S(1)} %bitcast.50, bf16[16,2,256,256]{3,2,1,0:T(8,128)(2,1)S(1)} %bitcast.42, s32[]{:T(128)S(6)} %select_n.42), kind=kOutput, calls=%fused_computation.6 | convolution fusion | flops 1073741824 | bytes 6815748 | tf_op jit(solution)/shard_map/dot_general | solution.py:14
  108.4 0.0 collective-permute-done.1
  108.4 0.1 add_convert_fusion
  108.5 0.8 copy.30
  (14 shorter events, 0.2 us)
Async XLA Ops:
  6.5 51.9 %copy-start.1 = (bf16[512,256]{1,0:T(8,128)(2,1)S(1)}, bf16[512,256]{1,0:T(8,128)(2,1)}, u32[]{:S(2)}) copy-start(bf16[512,256]{1,0:T(8,128)(2,1)} %param.5) | copy-start | bytes 786436
  6.5 23.2 %copy-start.2 = (s32[512,1]{0,1:T(1,128)S(1)}, s32[512,1]{0,1:T(1,128)}, u32[]{:S(2)}) copy-start(s32[512,1]{0,1:T(1,128)} %param.9) | copy-start | bytes 6148
  6.5 88.4 %all-gather.5.cloned.1.call-start = ((), (), s32[]{:S(2)}) async-start(), calls=%async_computation.1 | async-start | bytes 4456448 | tf_op jit(solution)/shard_map/all_gather | solution.py:32
  10.3 84.7 %collective-permute-start = (bf16[16,256,256]{2,1,0:T(8,128)(2,1)S(1)}, bf16[16,256,256]{2,1,0:T(8,128)(2,1)}, u32[]{:S(2)}, u32[]{:S(2)}) collective-permute-start(bf16[16,256,256]{2,1,0:T(8,128)(2,1)S(1)} %dynamic-slice_bitcast_fusion), channel_id=1, source_target_pairs={{0,1},{1,0},{2,3},{3,2},{4,5},{5,4},{6,7},{7,6},{8,9},{9,8},{10,11... | collective-permute-start | bytes 6291464 | tf_op jit(solution)/shard_map/ppermute | solution.py:55
  19.7 26.9 %all-to-all-start = ((bf16[32,8,256]{2,1,0:T(8,128)(2,1)}), bf16[32,8,256]{2,1,0:T(8,128)(2,1)S(1)}, u32[]{:S(2)}, u32[]{:S(2)}) async-start(bf16[32,8,256]{2,1,0:T(8,128)(2,1)} %copy.27), calls=%async_computation | async-start | bytes 262144 | tf_op jit(solution)/shard_map/all_to_all | solution.py:45
  58.8 6.1 %collective-permute-start.2 = (f32[16,512]{1,0:T(8,128)S(1)}, f32[16,512]{1,0:T(8,128)S(1)}, u32[]{:S(2)}, u32[]{:S(2)}) collective-permute-start(f32[16,512]{1,0:T(8,128)S(1)} %fusion.3), channel_id=1, source_target_pairs={{0,1},{1,0},{2,3},{3,2},{4,5},{5,4},{6,7},{7,6},{8,9},{9,8},{10,11... | collective-permute-start | bytes 98312 | tf_op jit(solution)/shard_map/ppermute | solution.py:65
  95.0 12.1 %copy-start = (bf16[8192,256]{1,0:T(8,128)(2,1)S(1)}, bf16[8192,256]{1,0:T(8,128)(2,1)}, u32[]{:S(2)}) copy-start(bf16[8192,256]{1,0:T(8,128)(2,1)} %param.6) | copy-start | bytes 12582916
  95.0 12.1 %copy-start.3 = (bf16[8192,256]{1,0:T(8,128)(2,1)S(1)}, bf16[8192,256]{1,0:T(8,128)(2,1)}, u32[]{:S(2)}) copy-start(bf16[8192,256]{1,0:T(8,128)(2,1)} %all-gather.5.cloned.1.call-done) | copy-start | bytes 12582916
  99.3 9.1 %collective-permute-start.1 = (f32[512,256]{0,1:T(8,128)S(1)}, f32[512,256]{0,1:T(8,128)S(1)}, u32[]{:S(2)}, u32[]{:S(2)}) collective-permute-start(f32[512,256]{0,1:T(8,128)S(1)} %convolution_bitcast_fusion), channel_id=1, source_target_pairs={{0,1},{1,0},{2,3},{3,2},{4,5},{5,4},{6,7},{7,6},{8,9},{9,8},{10,11... | collective-permute-start | bytes 1572872 | tf_op jit(solution)/shard_map/ppermute | solution.py:81
Sparse Core Ops, SparseCore 0:
  9.4 82.4 all-gather.4

commit v3 on v2

--- a/solution.py
+++ b/solution.py
@@ -1,8 +1,6 @@
 import jax
 import jax.numpy as jnp
 from jax import lax
-from jax.experimental import pallas as pl
-from jax.experimental.pallas import tpu as pltpu
 from jax.experimental.layout import Layout, with_layout_constraint
 from jax.sharding import PartitionSpec as P
 
@@ -12,13 +10,13 @@
 
 def _block_sum(x, w):
     return lax.dot_general(
-        x, w, (((0, 2), (0, 1)), ((), ())), preferred_element_type=jnp.float32
+        w, x, (((0, 1), (0, 2)), ((), ())), preferred_element_type=jnp.float32
     )
 
 
 def shards(tokens, query_base_weight, adapter_down_weight, adapter_up_weight, row_adapter_index):
     rows, width = tokens.shape
-    total_width, cols = query_base_weight.shape
+    _, cols = query_base_weight.shape
     groups = lax.axis_size("adp")
     chips = groups // 2
     rank = adapter_down_weight.shape[1]
@@ -41,7 +39,6 @@
         ]
     )
     pieces = pieces.reshape(2 * share, groups, width).transpose(1, 0, 2)
-    pieces, query_base_weight = lax.optimization_barrier((pieces, query_base_weight))
     pieces = lax.all_to_all(pieces, "adp", split_axis=0, concat_axis=0, tiled=True)
     pieces = pieces.reshape(adapters, 2, share, width).transpose(1, 2, 0, 3)
     lines = [[near * y + x for x in range(near)] for y in range(lax.axis_size("row") // near)]
@@ -51,6 +48,8 @@
 
     by_core = query_base_weight.reshape(chips, 2, width, cols)
     theirs = lax.dynamic_slice_in_dim(by_core, 1 - core, 1, 1)[:, 0]
+    mine = lax.dynamic_slice_in_dim(by_core, core, 1, 1)[:, 0]
+    mine, theirs = lax.optimization_barrier((mine, theirs))
     theirs = with_layout_constraint(theirs, Layout(major_to_minor=(0, 1, 2)))
     partner = lax.ppermute(theirs, "adp", swap)
     partner = with_layout_constraint(partner, Layout(major_to_minor=(0, 1, 2)))
@@ -68,8 +67,8 @@
     spread = jnp.where(chosen[None], ranks[:, None, :], jnp.zeros((), jnp.bfloat16))
     update = (
         lax.dot_general(
+            up,
             spread.reshape(rank * adapters, rows),
-            up,
             (((0,), (0,)), ((), ())),
             preferred_element_type=jnp.float32,
         )
@@ -79,8 +78,8 @@
 
     other = _block_sum(gathered, partner)
     other = lax.ppermute(other, "adp", swap)
-    own = _block_sum(gathered, lax.dynamic_slice_in_dim(by_core, core, 1, 1)[:, 0])
-    return (own + other + update.astype(jnp.float32)).astype(jnp.bfloat16)
+    own = _block_sum(gathered, mine)
+    return (own + other + update.astype(jnp.float32)).astype(jnp.bfloat16).T
 
 
 def solution(mesh):

time: 117 us -> 118 us (level)
  local copies, waits for them, and re-layouts: 4.5 us -> 9.1 us
  starting transfers between devices: 31.4 us -> 28.1 us
  waiting for transfers between devices: 18.4 us -> 20 us
    dynamic_slice x0 -> x1, local copies, waits for them, and re-layouts: none -> 2.42 us  [shards(): mine = lax.dynamic_slice_in_dim(by_core, core, 1, 1)[:, 0]]
    ppermute x1, starting transfers between devices: 7.4 us -> 5.22 us  [shards(): other = lax.ppermute(other, 'adp', swap)]
    squeeze x1, local copies, waits for them, and re-layouts: 1.74 us -> 3.92 us  [shards(): theirs = lax.dynamic_slice_in_dim(by_core, 1 - core, 1, 1)[:, 0]]
    all_to_all x1, waiting for transfers between devices: 16.8 us -> 18.5 us  [shards(): lax.all_to_all(pieces, 'adp', split_axis=0, concat_axis=0, tiled=True)]
    transpose x0 -> x2, local copies, waits for them, and re-layouts: none -> 1.57 us  [the longest x1 0.84 us: shards(): return (own + other + update.astype(jnp.float32)).astype(jnp.bfloat16).T]
    ppermute x1, starting transfers between devices: 5.24 us -> 4.01 us  [shards(): sums = sums + lax.ppermute(sums, 'adp', swap)]
  transfers between devices with their start and end apart: 5 -> 5, of which waited for: 2 -> 2; matrix products, arithmetic and copies ran while one was open for 5% -> 9% of each run, Pallas kernels for 0% -> 0%
where the time goes in v3:
time: 118 us; the launch traced here: 117 us
  blocking collectives  40.7 us (34%)
  starting transfers between devices  28.1 us (24%)
  waiting for transfers between devices  20 us (17%)
  between operations  13.6 us (12%)
  local copies, waits for them, and re-layouts  9.1 us (8%)
  matrix products  5.56 us (5%)
    all_gather x1, blocking collectives, shards(): lax.all_gather(sums, 'adp', axis=0, tiled=False, axis_index_groups=same_c...  29.2 us
    all_to_all x1, waiting for transfers between devices, shards(): lax.all_to_all(pieces, 'adp', split_axis=0, concat_axis=0, tiled=True)  18.5 us
    all_gather x1, blocking collectives, shards(): lax.all_gather(pieces, 'row', axis=0, tiled=False, axis_index_groups=lines)  11.5 us
    all_to_all x1, starting transfers between devices, shards(): lax.all_to_all(pieces, 'adp', split_axis=0, concat_axis=0, tiled=True)  10 us
    ppermute x1, starting transfers between devices, shards(): partner = lax.ppermute(theirs, 'adp', swap)  8.87 us
    ppermute x1, starting transfers between devices, shards(): other = lax.ppermute(other, 'adp', swap)  5.22 us
    dot_general x2, matrix products, _block_sum(): lax.dot_general(w, x, (((0, 1), (0, 2)), ((), ())), preferred_element_typ...  4.9 us
    ppermute x1, starting transfers between devices, shards(): sums = sums + lax.ppermute(sums, 'adp', swap)  4.01 us
  transfers between devices with their start and end apart: 5, of which 2 were waited for; matrix products, arithmetic and copies ran while one was open for 9% of the time, Pallas kernels for 0%

profile of v3, /device:TPU:1, one launch (start us, length us, event | category | flops | bytes accessed | tf_op | source)
XLA Modules:
  0.0 117.4 jit_solution(2394763946731504642)
XLA Ops:
  6.5 0.7 all-gather.5.cloned.1.call-update
  7.3 3.9 %dynamic-slice_bitcast_fusion = (bf16[16,256,256]{2,1,0:T(8,128)(2,1)}, bf16[16,1,256,256]{3,2,1,0:T(8,128)(2,1)S(1)}) fusion(bf16[16,2,256,256]{3,2,1,0:T(8,128)(2,1)} %bitcast.33, s32[]{:T(128)S(6)} %select_n.41, s32[]{:T(128)S(6)} %select_n.40), kind=kLoop, calls=%fused_computation | loop fusion | bytes 8388616 | tf_op jit(solution)/shard_map/squeeze | solution.py:50
  11.2 2.4 %copy.21 = bf16[16,1,256,256]{2,3,0,1:T(8,128)(2,1)} copy(bf16[16,1,256,256]{3,2,1,0:T(8,128)(2,1)S(1)} %get-tuple-element.10) | data formatting | bytes 4194304 | tf_op jit(solution)/shard_map/dynamic_slice | solution.py:51
  13.6 8.9 %collective-permute-start = (bf16[16,256,256]{2,1,0:T(8,128)(2,1)}, bf16[16,256,256]{2,1,0:T(8,128)(2,1)S(1)}, u32[]{:S(2)}, u32[]{:S(2)}) collective-permute-start(bf16[16,256,256]{2,1,0:T(8,128)(2,1)} %get-tuple-element.8), channel_id=1, source_target_pairs={{0,1},{1,0},{2,3},{3,2},{4,5},{5,4},{6,7},{7,6},{8,9},{9,8},{10,11... | collective-permute-start | bytes 6291464 | tf_op jit(solution)/shard_map/ppermute | solution.py:54
  22.5 1.0 constant_dynamic-slice_fusion
  23.6 0.1 pad_maximum_fusion
  23.7 0.1 reshape.57
  23.7 0.7 copy.23
  24.5 10.0 %all-to-all-start = ((bf16[32,8,256]{2,1,0:T(8,128)(2,1)}), bf16[32,8,256]{2,1,0:T(8,128)(2,1)S(1)}, u32[]{:S(2)}, u32[]{:S(2)}) async-start(bf16[32,8,256]{2,1,0:T(8,128)(2,1)} %copy.23), calls=%async_computation | async-start | bytes 262144 | tf_op jit(solution)/shard_map/all_to_all | solution.py:42
  34.5 18.5 %all-to-all-done = bf16[32,8,256]{2,1,0:T(8,128)(2,1)S(1)} async-done(((bf16[32,8,256]{2,1,0:T(8,128)(2,1)}), bf16[32,8,256]{2,1,0:T(8,128)(2,1)S(1)}, u32[]{:S(2)}, u32[]{:S(2)}) %all-to-all-start) | async-done | bytes 131104 | tf_op jit(solution)/shard_map/all_to_all | solution.py:42
  53.0 11.5 %all-gather.1 = bf16[8,4,32,256]{3,2,1,0:T(8,128)(2,1)S(1)} all-gather(bf16[2,4,32,256]{3,2,1,0:T(8,128)(2,1)S(1)} %bitcast.37), channel_id=3, replica_groups={{0,32,64,96},{128,160,192,224},{256,288,320,352},{384,416,448,480},{1,3..., dimensions={0}, use_global_device_ids=true | all-gather | bytes 655360 | tf_op jit(solution)/shard_map/all_gather | solution.py:45
  64.6 0.3 fusion
  64.9 4.0 %collective-permute-start.2 = (f32[16,512]{1,0:T(8,128)S(1)}, f32[16,512]{1,0:T(8,128)S(1)}, u32[]{:S(2)}, u32[]{:S(2)}) collective-permute-start(f32[16,512]{1,0:T(8,128)S(1)} %fusion), channel_id=1, source_target_pairs={{0,1},{1,0},{2,3},{3,2},{4,5},{5,4},{6,7},{7,6},{8,9},{9,8},{10,11... | collective-permute-start | bytes 98312 | tf_op jit(solution)/shard_map/ppermute | solution.py:64
  68.9 0.8 collective-permute-done.2
  69.8 29.2 %all-gather.2 = f32[256,512]{1,0:T(8,128)S(1)} all-gather(f32[16,512]{1,0:T(8,128)S(1)} %add.33), channel_id=4, replica_groups={{0,2,4,6,8,10,12,14,16,18,20,22,24,26,28,30},{1,3,5,7,9,11,13,15,17,19,..., dimensions={0}, use_global_device_ids=true | all-gather | bytes 557056 | tf_op jit(solution)/shard_map/all_gather | solution.py:65
  99.0 0.0 collective-permute-done
  99.1 0.0 all-gather.5.cloned.1.call-done
  99.1 3.6 %convolution_bitcast_fusion = f32[256,512]{1,0:T(8,128)S(1)} fusion(bf16[16,256,256]{2,1,0:T(8,128)(2,1)S(1)} %collective-permute-done, bf16[16,512,256]{2,1,0:T(8,128)(2,1)} %bitcast.43), kind=kOutput, calls=%fused_computation.3 | convolution fusion | flops 1073741824 | bytes 6815744 | tf_op jit(solution)/shard_map/dot_general | solution.py:12
  102.7 5.2 %collective-permute-start.1 = (f32[256,512]{1,0:T(8,128)S(1)}, f32[256,512]{1,0:T(8,128)S(1)}, u32[]{:S(2)}, u32[]{:S(2)}) collective-permute-start(f32[256,512]{1,0:T(8,128)S(1)} %convolution_bitcast_fusion), channel_id=1, source_target_pairs={{0,1},{1,0},{2,3},{3,2},{4,5},{5,4},{6,7},{7,6},{8,9},{9,8},{10,11... | collective-permute-start | bytes 1572872 | tf_op jit(solution)/shard_map/ppermute | solution.py:80
  108.0 0.3 fusion.1
  108.3 1.3 %convolution_bitcast_fusion.1 = f32[256,512]{1,0:T(8,128)S(1)} fusion(bf16[16,256,256]{1,2,0:T(8,128)(2,1)S(1)} %bitcast.35, bf16[16,512,256]{2,1,0:T(8,128)(2,1)S(1)} %bitcast.44), kind=kOutput, calls=%fused_computation.4 | convolution fusion | flops 1073741824 | bytes 6815744 | tf_op jit(solution)/shard_map/dot_general | solution.py:12
  109.6 0.0 collective-permute-done.1
  109.6 0.1 fusion.2
  109.7 0.8 copy.25
  (15 shorter events, 0.2 us)
Async XLA Ops:
  6.5 92.5 %all-gather.5.cloned.1.call-start = ((), (), s32[]{:S(2)}) async-start(), calls=%async_computation.1 | async-start | bytes 4456448 | tf_op jit(solution)/shard_map/all_gather | solution.py:30
  11.2 23.3 %copy-start.2 = (s32[512,1]{0,1:T(1,128)S(1)}, s32[512,1]{0,1:T(1,128)}, u32[]{:S(2)}) copy-start(s32[512,1]{0,1:T(1,128)} %param.9) | copy-start | bytes 6148
  13.6 50.9 %copy-start.1 = (bf16[512,256]{1,0:T(8,128)(2,1)S(1)}, bf16[512,256]{1,0:T(8,128)(2,1)}, u32[]{:S(2)}) copy-start(bf16[512,256]{1,0:T(8,128)(2,1)} %param.5) | copy-start | bytes 786436
  13.6 85.4 %collective-permute-start = (bf16[16,256,256]{2,1,0:T(8,128)(2,1)}, bf16[16,256,256]{2,1,0:T(8,128)(2,1)S(1)}, u32[]{:S(2)}, u32[]{:S(2)}) collective-permute-start(bf16[16,256,256]{2,1,0:T(8,128)(2,1)} %get-tuple-element.8), channel_id=1, source_target_pairs={{0,1},{1,0},{2,3},{3,2},{4,5},{5,4},{6,7},{7,6},{8,9},{9,8},{10,11... | collective-permute-start | bytes 6291464 | tf_op jit(solution)/shard_map/ppermute | solution.py:54
  24.5 28.5 %all-to-all-start = ((bf16[32,8,256]{2,1,0:T(8,128)(2,1)}), bf16[32,8,256]{2,1,0:T(8,128)(2,1)S(1)}, u32[]{:S(2)}, u32[]{:S(2)}) async-start(bf16[32,8,256]{2,1,0:T(8,128)(2,1)} %copy.23), calls=%async_computation | async-start | bytes 262144 | tf_op jit(solution)/shard_map/all_to_all | solution.py:42
  64.9 4.9 %collective-permute-start.2 = (f32[16,512]{1,0:T(8,128)S(1)}, f32[16,512]{1,0:T(8,128)S(1)}, u32[]{:S(2)}, u32[]{:S(2)}) collective-permute-start(f32[16,512]{1,0:T(8,128)S(1)} %fusion), channel_id=1, source_target_pairs={{0,1},{1,0},{2,3},{3,2},{4,5},{5,4},{6,7},{7,6},{8,9},{9,8},{10,11... | collective-permute-start | bytes 98312 | tf_op jit(solution)/shard_map/ppermute | solution.py:64
  99.1 9.2 %copy-start = (bf16[16,1,256,256]{2,3,0,1:T(8,128)(2,1)S(1)}, bf16[16,1,256,256]{2,3,0,1:T(8,128)(2,1)}, u32[]{:S(2)}) copy-start(bf16[16,1,256,256]{2,3,0,1:T(8,128)(2,1)} %copy.21) | copy-start | bytes 6291460
  99.1 9.2 %copy-start.3 = (bf16[8192,256]{1,0:T(8,128)(2,1)S(1)}, bf16[8192,256]{1,0:T(8,128)(2,1)}, u32[]{:S(2)}) copy-start(bf16[8192,256]{1,0:T(8,128)(2,1)} %all-gather.5.cloned.1.call-done) | copy-start | bytes 12582916
  102.7 6.9 %collective-permute-start.1 = (f32[256,512]{1,0:T(8,128)S(1)}, f32[256,512]{1,0:T(8,128)S(1)}, u32[]{:S(2)}, u32[]{:S(2)}) collective-permute-start(f32[256,512]{1,0:T(8,128)S(1)} %convolution_bitcast_fusion), channel_id=1, source_target_pairs={{0,1},{1,0},{2,3},{3,2},{4,5},{5,4},{6,7},{7,6},{8,9},{9,8},{10,11... | collective-permute-start | bytes 1572872 | tf_op jit(solution)/shard_map/ppermute | solution.py:80
Sparse Core Ops, SparseCore 0:
  9.4 82.5 all-gather.4

commit v4 on v3

--- a/solution.py
+++ b/solution.py
@@ -9,9 +9,10 @@
 
 
 def _block_sum(x, w):
-    return lax.dot_general(
-        w, x, (((0, 1), (0, 2)), ((), ())), preferred_element_type=jnp.float32
+    y = lax.dot_general(
+        x, w, (((0, 2), (0, 1)), ((), ())), preferred_element_type=jnp.float32
     )
+    return with_layout_constraint(y, Layout(major_to_minor=(0, 1)))
 
 
 def shards(tokens, query_base_weight, adapter_down_weight, adapter_up_weight, row_adapter_index):
@@ -21,10 +22,10 @@
     chips = groups // 2
     rank = adapter_down_weight.shape[1]
     adapters = groups
-    core = lax.axis_index("adp") % 2
+    core = (lax.axis_index("adp") + lax.axis_index("adp") // 2) % 2
     row = lax.axis_index("row")
     scale = SCALE_NUMERATOR / ADAPTER_RANK
-    same_core = [[2 * z + c for z in range(chips)] for c in range(2)]
+    same_core = [[2 * z + (z + c) % 2 for z in range(chips)] for c in range(2)]
     swap = [(a, a ^ 1) for a in range(groups)]
 
     gathered = lax.all_gather(tokens, "adp", axis=0, tiled=False, axis_index_groups=same_core)
@@ -46,10 +47,13 @@
     down = pieces[:, 0].reshape(rank * adapters, width)
     up = pieces[:, 1].reshape(rank * adapters, cols)
 
-    by_core = query_base_weight.reshape(chips, 2, width, cols)
-    theirs = lax.dynamic_slice_in_dim(by_core, 1 - core, 1, 1)[:, 0]
-    mine = lax.dynamic_slice_in_dim(by_core, core, 1, 1)[:, 0]
+    by_core = query_base_weight.reshape(chips // 2, 2, 2, width, cols)
+    plain = (jnp.arange(2, dtype=jnp.int32) == core)[None, :, None, None]
+    theirs = jnp.where(plain, by_core[:, :, 1], by_core[:, :, 0])
+    mine = jnp.where(plain, by_core[:, :, 0], by_core[:, :, 1])
     mine, theirs = lax.optimization_barrier((mine, theirs))
+    mine = mine.reshape(chips, width, cols)
+    theirs = theirs.reshape(chips, width, cols)
     theirs = with_layout_constraint(theirs, Layout(major_to_minor=(0, 1, 2)))
     partner = lax.ppermute(theirs, "adp", swap)
     partner = with_layout_constraint(partner, Layout(major_to_minor=(0, 1, 2)))
@@ -67,19 +71,20 @@
     spread = jnp.where(chosen[None], ranks[:, None, :], jnp.zeros((), jnp.bfloat16))
     update = (
         lax.dot_general(
+            spread.reshape(rank * adapters, rows),
             up,
-            spread.reshape(rank * adapters, rows),
             (((0,), (0,)), ((), ())),
             preferred_element_type=jnp.float32,
         )
         * scale
     ).astype(jnp.bfloat16)
     update = lax.optimization_barrier(update)
+    update = with_layout_constraint(update, Layout(major_to_minor=(0, 1)))
 
     other = _block_sum(gathered, partner)
     other = lax.ppermute(other, "adp", swap)
     own = _block_sum(gathered, mine)
-    return (own + other + update.astype(jnp.float32)).astype(jnp.bfloat16).T
+    return (own + other + update.astype(jnp.float32)).astype(jnp.bfloat16)
 
 
 def solution(mesh):

time: 118 us -> 115 us (0.975)
  local copies, waits for them, and re-layouts: 9.1 us -> 1.92 us
  other arithmetic: 0.33 us -> 4.89 us
  blocking collectives: 40.7 us -> 42.4 us
    squeeze x1 -> x0, local copies, waits for them, and re-layouts: 3.92 us -> none  [shards(): theirs = lax.dynamic_slice_in_dim(by_core, 1 - core, 1, 1)[:, 0]]
    select_n x0 -> x1, other arithmetic: none -> 3.9 us  [shards(): theirs = jnp.where(plain, by_core[:, :, 1], by_core[:, :, 0])]
    dynamic_slice x1 -> x0, local copies, waits for them, and re-layouts: 2.42 us -> none  [shards(): mine = lax.dynamic_slice_in_dim(by_core, core, 1, 1)[:, 0]]
    ppermute x1, starting transfers between devices: 5.22 us -> 3.87 us  [shards(): other = lax.ppermute(other, 'adp', swap)]
  transfers between devices with their start and end apart: 5 -> 5, of which waited for: 2 -> 2; matrix products, arithmetic and copies ran while one was open for 9% -> 7% of each run, Pallas kernels for 0% -> 0%
where the time goes in v4:
time: 115 us
  blocking collectives  42.4 us (37%)
  starting transfers between devices  27.1 us (24%)
  waiting for transfers between devices  19 us (17%)
  between operations  13.6 us (12%)
  matrix products  6.21 us (5%)
  other arithmetic  4.89 us (4%)
  local copies, waits for them, and re-layouts  1.92 us (2%)
    all_gather x1, blocking collectives, shards(): lax.all_gather(sums, 'adp', axis=0, tiled=False, axis_index_groups=same_c...  30.1 us
    all_to_all x1, waiting for transfers between devices, shards(): lax.all_to_all(pieces, 'adp', split_axis=0, concat_axis=0, tiled=True)  17.4 us
    all_gather x1, blocking collectives, shards(): lax.all_gather(pieces, 'row', axis=0, tiled=False, axis_index_groups=lines)  12.2 us
    all_to_all x1, starting transfers between devices, shards(): lax.all_to_all(pieces, 'adp', split_axis=0, concat_axis=0, tiled=True)  10 us
    ppermute x1, starting transfers between devices, shards(): partner = lax.ppermute(theirs, 'adp', swap)  8.87 us
    dot_general x2, matrix products, _block_sum(): lax.dot_general(x, w, (((0, 2), (0, 1)), ((), ())), preferred_element_typ...  5.52 us
    ppermute x1, starting transfers between devices, shards(): sums = sums + lax.ppermute(sums, 'adp', swap)  4.32 us
    select_n x1, other arithmetic, shards(): theirs = jnp.where(plain, by_core[:, :, 1], by_core[:, :, 0])  3.9 us
  transfers between devices with their start and end apart: 5, of which 2 were waited for; matrix products, arithmetic and copies ran while one was open for 7% of the time, Pallas kernels for 0%

profile of v4, /device:TPU:1, one launch (start us, length us, event | category | flops | bytes accessed | tf_op | source)
XLA Modules:
  0.0 115.1 jit_solution(16800255719529408048)
XLA Ops:
  6.5 0.0 all-gather.5.cloned.1.call-start
  6.5 0.7 all-gather.5.cloned.1.call-update
  7.3 0.0 copy-start.1
  7.3 3.9 %broadcast_select_fusion = (bf16[8,2,256,256]{3,2,1,0:T(8,128)(2,1)}, bf16[8,2,256,256]{3,2,1,0:T(8,128)(2,1)S(1)}) fusion(pred[2]{0:T(512)(128)(4,1)S(1)} %iota_compare_fusion.1, bf16[8,2,2,256,256]{4,3,2,1,0:T(8,128)(2,1)} %bitcast.48), kind=kLoop, calls=%fused_computation.2 | loop fusion | flops 2097152 | bytes 8388610 | tf_op jit(solution)/shard_map/jit(_where)/select_n | solution.py:52
  11.2 8.9 %collective-permute-start = (bf16[16,256,256]{2,1,0:T(8,128)(2,1)}, bf16[16,256,256]{2,1,0:T(8,128)(2,1)}, u32[]{:S(2)}, u32[]{:S(2)}) collective-permute-start(bf16[16,256,256]{2,1,0:T(8,128)(2,1)} %bitcast.7), channel_id=1, source_target_pairs={{0,1},{1,0},{2,3},{3,2},{4,5},{5,4},{6,7},{7,6},{8,9},{9,8},{10,11... | collective-permute-start | bytes 6291464 | tf_op jit(solution)/shard_map/ppermute | solution.py:58
  20.1 1.0 constant_dynamic-slice_fusion
  21.1 0.1 pad_maximum_fusion
  21.2 0.1 reshape.69
  21.3 0.7 copy.19
  22.1 10.0 %all-to-all-start = ((bf16[32,8,256]{2,1,0:T(8,128)(2,1)}), bf16[32,8,256]{2,1,0:T(8,128)(2,1)S(1)}, u32[]{:S(2)}, u32[]{:S(2)}) async-start(bf16[32,8,256]{2,1,0:T(8,128)(2,1)} %copy.19), calls=%async_computation | async-start | bytes 262144 | tf_op jit(solution)/shard_map/all_to_all | solution.py:43
  32.1 17.4 %all-to-all-done = bf16[32,8,256]{2,1,0:T(8,128)(2,1)S(1)} async-done(((bf16[32,8,256]{2,1,0:T(8,128)(2,1)}), bf16[32,8,256]{2,1,0:T(8,128)(2,1)S(1)}, u32[]{:S(2)}, u32[]{:S(2)}) %all-to-all-start) | async-done | bytes 131104 | tf_op jit(solution)/shard_map/all_to_all | solution.py:43
  49.6 12.2 %all-gather.1 = bf16[8,4,32,256]{3,2,1,0:T(8,128)(2,1)S(1)} all-gather(bf16[2,4,32,256]{3,2,1,0:T(8,128)(2,1)S(1)} %bitcast.52), channel_id=3, replica_groups={{0,32,64,96},{128,160,192,224},{256,288,320,352},{384,416,448,480},{1,3..., dimensions={0}, use_global_device_ids=true | all-gather | bytes 655360 | tf_op jit(solution)/shard_map/all_gather | solution.py:46
  61.9 0.3 fusion
  62.2 4.3 %collective-permute-start.2 = (f32[16,512]{1,0:T(8,128)S(1)}, f32[16,512]{1,0:T(8,128)S(1)}, u32[]{:S(2)}, u32[]{:S(2)}) collective-permute-start(f32[16,512]{1,0:T(8,128)S(1)} %fusion), channel_id=1, source_target_pairs={{0,1},{1,0},{2,3},{3,2},{4,5},{5,4},{6,7},{7,6},{8,9},{9,8},{10,11... | collective-permute-start | bytes 98312 | tf_op jit(solution)/shard_map/ppermute | solution.py:68
  66.5 0.8 collective-permute-done.2
  67.4 30.1 %all-gather.2 = f32[256,512]{1,0:T(8,128)S(1)} all-gather(f32[16,512]{1,0:T(8,128)S(1)} %add.29), channel_id=4, replica_groups={{0,3,4,7,8,11,12,15,16,19,20,23,24,27,28,31},{1,2,5,6,9,10,13,14,17,18,..., dimensions={0}, use_global_device_ids=true | all-gather | bytes 557056 | tf_op jit(solution)/shard_map/all_gather | solution.py:69
  97.6 0.0 collective-permute-done
  97.6 0.0 all-gather.5.cloned.1.call-done
  97.7 4.2 %convolution_bitcast_fusion = f32[512,256]{1,0:T(8,128)S(1)} fusion(bf16[16,512,256]{2,1,0:T(8,128)(2,1)} %bitcast.58, bf16[16,256,256]{2,1,0:T(8,128)(2,1)} %collective-permute-done), kind=kOutput, calls=%fused_computation.6 | convolution fusion | flops 1073741824 | bytes 6815744 | tf_op jit(solution)/shard_map/dot_general | solution.py:12
  101.9 3.9 %collective-permute-start.1 = (f32[512,256]{1,0:T(8,128)S(1)}, f32[512,256]{1,0:T(8,128)S(1)}, u32[]{:S(2)}, u32[]{:S(2)}) collective-permute-start(f32[512,256]{1,0:T(8,128)S(1)} %convolution_bitcast_fusion), channel_id=1, source_target_pairs={{0,1},{1,0},{2,3},{3,2},{4,5},{5,4},{6,7},{7,6},{8,9},{9,8},{10,11... | collective-permute-start | bytes 1572872 | tf_op jit(solution)/shard_map/ppermute | solution.py:85
  105.8 0.3 fusion.1
  106.2 1.3 %convolution_bitcast_fusion.1 = f32[512,256]{1,0:T(8,128)S(1)} fusion(bf16[16,512,256]{2,1,0:T(8,128)(2,1)S(1)} %bitcast.59, bf16[16,256,256]{2,1,0:T(8,128)(2,1)S(1)} %bitcast.51), kind=kOutput, calls=%fused_computation.7 | convolution fusion | flops 1073741824 | bytes 6815744 | tf_op jit(solution)/shard_map/dot_general | solution.py:12
  107.4 0.0 collective-permute-done.1
  107.4 0.8 add_convert_fusion
  (12 shorter events, 0.2 us)
Async XLA Ops:
  6.5 91.1 %all-gather.5.cloned.1.call-start = ((), (), s32[]{:S(2)}) async-start(), calls=%async_computation.1 | async-start | bytes 4456448 | tf_op jit(solution)/shard_map/all_gather | solution.py:31
  7.3 24.8 %copy-start.1 = (s32[512,1]{0,1:T(1,128)S(1)}, s32[512,1]{0,1:T(1,128)}, u32[]{:S(2)}) copy-start(s32[512,1]{0,1:T(1,128)} %param.9) | copy-start | bytes 6148
  11.2 50.6 %copy-start = (bf16[512,256]{1,0:T(8,128)(2,1)S(1)}, bf16[512,256]{1,0:T(8,128)(2,1)}, u32[]{:S(2)}) copy-start(bf16[512,256]{1,0:T(8,128)(2,1)} %param.5) | copy-start | bytes 786436
  11.2 86.4 %collective-permute-start = (bf16[16,256,256]{2,1,0:T(8,128)(2,1)}, bf16[16,256,256]{2,1,0:T(8,128)(2,1)}, u32[]{:S(2)}, u32[]{:S(2)}) collective-permute-start(bf16[16,256,256]{2,1,0:T(8,128)(2,1)} %bitcast.7), channel_id=1, source_target_pairs={{0,1},{1,0},{2,3},{3,2},{4,5},{5,4},{6,7},{7,6},{8,9},{9,8},{10,11... | collective-permute-start | bytes 6291464 | tf_op jit(solution)/shard_map/ppermute | solution.py:58
  22.1 27.5 %all-to-all-start = ((bf16[32,8,256]{2,1,0:T(8,128)(2,1)}), bf16[32,8,256]{2,1,0:T(8,128)(2,1)S(1)}, u32[]{:S(2)}, u32[]{:S(2)}) async-start(bf16[32,8,256]{2,1,0:T(8,128)(2,1)} %copy.19), calls=%async_computation | async-start | bytes 262144 | tf_op jit(solution)/shard_map/all_to_all | solution.py:43
  62.2 5.2 %collective-permute-start.2 = (f32[16,512]{1,0:T(8,128)S(1)}, f32[16,512]{1,0:T(8,128)S(1)}, u32[]{:S(2)}, u32[]{:S(2)}) collective-permute-start(f32[16,512]{1,0:T(8,128)S(1)} %fusion), channel_id=1, source_target_pairs={{0,1},{1,0},{2,3},{3,2},{4,5},{5,4},{6,7},{7,6},{8,9},{9,8},{10,11... | collective-permute-start | bytes 98312 | tf_op jit(solution)/shard_map/ppermute | solution.py:68
  97.6 8.5 %copy-start.2 = (bf16[8192,256]{1,0:T(8,128)(2,1)S(1)}, bf16[8192,256]{1,0:T(8,128)(2,1)}, u32[]{:S(2)}) copy-start(bf16[8192,256]{1,0:T(8,128)(2,1)} %all-gather.5.cloned.1.call-done) | copy-start | bytes 12582916
  101.9 5.5 %collective-permute-start.1 = (f32[512,256]{1,0:T(8,128)S(1)}, f32[512,256]{1,0:T(8,128)S(1)}, u32[]{:S(2)}, u32[]{:S(2)}) collective-permute-start(f32[512,256]{1,0:T(8,128)S(1)} %convolution_bitcast_fusion), channel_id=1, source_target_pairs={{0,1},{1,0},{2,3},{3,2},{4,5},{5,4},{6,7},{7,6},{8,9},{9,8},{10,11... | collective-permute-start | bytes 1572872 | tf_op jit(solution)/shard_map/ppermute | solution.py:85
Sparse Core Ops, SparseCore 0:
  9.4 86.9 all-gather.4

commit v5 on v4

--- a/solution.py
+++ b/solution.py
@@ -51,7 +51,7 @@
     plain = (jnp.arange(2, dtype=jnp.int32) == core)[None, :, None, None]
     theirs = jnp.where(plain, by_core[:, :, 1], by_core[:, :, 0])
     mine = jnp.where(plain, by_core[:, :, 0], by_core[:, :, 1])
-    mine, theirs = lax.optimization_barrier((mine, theirs))
+    theirs, mine = lax.optimization_barrier((theirs, mine))
     mine = mine.reshape(chips, width, cols)
     theirs = theirs.reshape(chips, width, cols)
     theirs = with_layout_constraint(theirs, Layout(major_to_minor=(0, 1, 2)))
@@ -65,9 +65,13 @@
         down, tokens, (((1,), (1,)), ((), ())), preferred_element_type=jnp.float32
     ).reshape(rank, adapters, rows)
     sums = jnp.where(chosen[None], sums, 0.0).sum(axis=1)
-    sums = sums + lax.ppermute(sums, "adp", swap)
-    sums = lax.all_gather(sums, "adp", axis=0, tiled=False, axis_index_groups=same_core)
-    ranks = sums.sum(axis=0).astype(jnp.bfloat16)
+    pairs = [[a, a + 1] for a in range(0, groups, 2)]
+    sums = lax.all_gather(sums, "adp", axis=0, tiled=False, axis_index_groups=pairs).sum(axis=0)
+    part = rows // 2
+    sums = lax.dynamic_slice_in_dim(sums, (lax.axis_index("adp") % 2) * part, part, 1)
+    sums = lax.all_gather(sums, "adp", axis=0, tiled=False)
+    sums = sums.reshape(chips, 2, rank, part).sum(axis=0)
+    ranks = sums.transpose(1, 0, 2).reshape(rank, rows).astype(jnp.bfloat16)
     spread = jnp.where(chosen[None], ranks[:, None, :], jnp.zeros((), jnp.bfloat16))
     update = (
         lax.dot_general(
@@ -78,7 +82,7 @@
         )
         * scale
     ).astype(jnp.bfloat16)
-    update = lax.optimization_barrier(update)
+    update, gathered = lax.optimization_barrier((update, gathered))
     update = with_layout_constraint(update, Layout(major_to_minor=(0, 1)))
 
     other = _block_sum(gathered, partner)

time: 115 us -> 113 us (0.983)
  starting transfers between devices: 27.1 us -> 21 us
  blocking collectives: 42.4 us -> 46.6 us
    ppermute x1 -> x0, starting transfers between devices: 4.32 us -> none  [shards(): sums = sums + lax.ppermute(sums, 'adp', swap)]
    all_gather x1 -> x2, blocking collectives: 30.1 us -> 34.4 us  [the longest x1 30.4 us: shards(): sums = lax.all_gather(sums, 'adp', axis=0, tiled=False)]
    ppermute x1, starting transfers between devices: 3.87 us -> 2.07 us  [shards(): other = lax.ppermute(other, 'adp', swap)]
  transfers between devices with their start and end apart: 5 -> 4, of which waited for: 2 -> 2; matrix products, arithmetic and copies ran while one was open for 7% -> 7% of each run, Pallas kernels for 0% -> 0%
where the time goes in v5:
time: 113 us
  blocking collectives  46.6 us (41%)
  starting transfers between devices  21 us (19%)
  waiting for transfers between devices  18.6 us (16%)
  between operations  13.6 us (12%)
  matrix products  6.2 us (5%)
  other arithmetic  4.89 us (4%)
  local copies, waits for them, and re-layouts  1.94 us (2%)
    all_gather x1, blocking collectives, shards(): sums = lax.all_gather(sums, 'adp', axis=0, tiled=False)  30.4 us
    all_to_all x1, waiting for transfers between devices, shards(): lax.all_to_all(pieces, 'adp', split_axis=0, concat_axis=0, tiled=True)  17.4 us
    all_gather x1, blocking collectives, shards(): lax.all_gather(pieces, 'row', axis=0, tiled=False, axis_index_groups=lines)  12.2 us
    all_to_all x1, starting transfers between devices, shards(): lax.all_to_all(pieces, 'adp', split_axis=0, concat_axis=0, tiled=True)  10 us
    ppermute x1, starting transfers between devices, shards(): partner = lax.ppermute(theirs, 'adp', swap)  8.87 us
    dot_general x2, matrix products, _block_sum(): lax.dot_general(x, w, (((0, 2), (0, 1)), ((), ())), preferred_element_typ...  5.52 us
    all_gather x1, blocking collectives, shards(): lax.all_gather(sums, 'adp', axis=0, tiled=False, axis_index_groups=pairs)  3.95 us
    select_n x1, other arithmetic, shards(): mine = jnp.where(plain, by_core[:, :, 0], by_core[:, :, 1])  3.9 us
  transfers between devices with their start and end apart: 4, of which 2 were waited for; matrix products, arithmetic and copies ran while one was open for 7% of the time, Pallas kernels for 0%

profile of v5, /device:TPU:1, one launch (start us, length us, event | category | flops | bytes accessed | tf_op | source)
XLA Modules:
  0.0 112.8 jit_solution(15692309056184310698)
XLA Ops:
  6.5 0.0 all-gather.6.cloned.1.call-start
  6.5 0.7 all-gather.6.cloned.1.call-update
  7.3 0.0 copy-start.1
  7.3 3.9 %broadcast_select_fusion = (bf16[8,2,256,256]{3,2,1,0:T(8,128)(2,1)S(1)}, bf16[8,2,256,256]{3,2,1,0:T(8,128)(2,1)}) fusion(pred[2]{0:T(512)(128)(4,1)S(1)} %iota_compare_fusion.1, bf16[8,2,2,256,256]{4,3,2,1,0:T(8,128)(2,1)} %bitcast.50), kind=kLoop, calls=%fused_computation.2 | loop fusion | flops 2097152 | bytes 8388610 | tf_op jit(solution)/shard_map/jit(_where)/select_n | solution.py:53
  11.2 8.9 %collective-permute-start = (bf16[16,256,256]{2,1,0:T(8,128)(2,1)}, bf16[16,256,256]{2,1,0:T(8,128)(2,1)}, u32[]{:S(2)}, u32[]{:S(2)}) collective-permute-start(bf16[16,256,256]{2,1,0:T(8,128)(2,1)} %bitcast.18), channel_id=1, source_target_pairs={{0,1},{1,0},{2,3},{3,2},{4,5},{5,4},{6,7},{7,6},{8,9},{9,8},{10,11... | collective-permute-start | bytes 6291464 | tf_op jit(solution)/shard_map/ppermute | solution.py:58
  20.1 1.0 constant_dynamic-slice_fusion.1
  21.1 0.1 pad_maximum_fusion
  21.2 0.1 reshape.73
  21.3 0.7 copy.21
  22.1 10.0 %all-to-all-start = ((bf16[32,8,256]{2,1,0:T(8,128)(2,1)}), bf16[32,8,256]{2,1,0:T(8,128)(2,1)S(1)}, u32[]{:S(2)}, u32[]{:S(2)}) async-start(bf16[32,8,256]{2,1,0:T(8,128)(2,1)} %copy.21), calls=%async_computation | async-start | bytes 262144 | tf_op jit(solution)/shard_map/all_to_all | solution.py:43
  32.1 0.0 copy-done.1
  32.1 17.4 %all-to-all-done = bf16[32,8,256]{2,1,0:T(8,128)(2,1)S(1)} async-done(((bf16[32,8,256]{2,1,0:T(8,128)(2,1)}), bf16[32,8,256]{2,1,0:T(8,128)(2,1)S(1)}, u32[]{:S(2)}, u32[]{:S(2)}) %all-to-all-start) | async-done | bytes 131104 | tf_op jit(solution)/shard_map/all_to_all | solution.py:43
  49.6 12.2 %all-gather = bf16[8,4,32,256]{3,2,1,0:T(8,128)(2,1)S(1)} all-gather(bf16[2,4,32,256]{3,2,1,0:T(8,128)(2,1)S(1)} %bitcast.54), channel_id=2, replica_groups={{0,32,64,96},{128,160,192,224},{256,288,320,352},{384,416,448,480},{1,3..., dimensions={0}, use_global_device_ids=true | all-gather | bytes 655360 | tf_op jit(solution)/shard_map/all_gather | solution.py:46
  61.8 0.3 fusion
  62.2 4.0 %all-gather.1 = f32[32,512]{1,0:T(8,128)S(1)} all-gather(f32[16,512]{1,0:T(8,128)S(1)} %fusion), channel_id=3, replica_groups={{0,1},{2,3},{4,5},{6,7},{8,9},{10,11},{12,13},{14,15},{16,17},{18,19},{..., dimensions={0}, use_global_device_ids=true | all-gather | bytes 98304 | tf_op jit(solution)/shard_map/all_gather | solution.py:69
  66.1 30.4 %all-gather.2 = f32[512,256]{1,0:T(8,128)S(1)} all-gather(f32[16,256]{1,0:T(8,128)S(1)} %constant_dynamic-slice_fusion), channel_id=4, replica_groups=mesh['row'=16,'adp'=32] {'adp'}, dimensions={0}, use_global_device_ids=true | all-gather | bytes 540672 | tf_op jit(solution)/shard_map/all_gather | solution.py:72
  96.7 0.3 fusion.1
  97.0 0.0 all-gather.6.cloned.1.call-done
  97.1 0.0 collective-permute-done
  97.1 4.2 %convolution_bitcast_fusion = f32[512,256]{1,0:T(8,128)S(1)} fusion(bf16[16,512,256]{2,1,0:T(8,128)(2,1)} %bitcast.63, bf16[16,256,256]{2,1,0:T(8,128)(2,1)} %collective-permute-done), kind=kOutput, calls=%fused_computation.6 | convolution fusion | flops 1073741824 | bytes 6815744 | tf_op jit(solution)/shard_map/dot_general | solution.py:12
  101.3 2.1 %collective-permute-start.1 = (f32[512,256]{1,0:T(8,128)S(1)}, f32[512,256]{1,0:T(8,128)S(1)}, u32[]{:S(2)}, u32[]{:S(2)}) collective-permute-start(f32[512,256]{1,0:T(8,128)S(1)} %convolution_bitcast_fusion), channel_id=1, source_target_pairs={{0,1},{1,0},{2,3},{3,2},{4,5},{5,4},{6,7},{7,6},{8,9},{9,8},{10,11... | collective-permute-start | bytes 1572872 | tf_op jit(solution)/shard_map/ppermute | solution.py:89
  103.4 1.3 %convolution_bitcast_fusion.1 = f32[512,256]{1,0:T(8,128)S(1)} fusion(bf16[16,512,256]{2,1,0:T(8,128)(2,1)S(1)} %bitcast.64, bf16[16,256,256]{2,1,0:T(8,128)(2,1)S(1)} %bitcast.53), kind=kOutput, calls=%fused_computation.7 | convolution fusion | flops 1073741824 | bytes 6815744 | tf_op jit(solution)/shard_map/dot_general | solution.py:12
  104.7 0.4 collective-permute-done.1
  105.1 0.8 add_convert_fusion
  (13 shorter events, 0.2 us)
Async XLA Ops:
  6.5 90.5 %all-gather.6.cloned.1.call-start = ((), (), s32[]{:S(2)}) async-start(), calls=%async_computation.1 | async-start | bytes 4456448 | tf_op jit(solution)/shard_map/all_gather | solution.py:31
  7.3 24.8 %copy-start.1 = (s32[512,1]{0,1:T(1,128)S(1)}, s32[512,1]{0,1:T(1,128)}, u32[]{:S(2)}) copy-start(s32[512,1]{0,1:T(1,128)} %param.9) | copy-start | bytes 6148
  11.2 50.6 %copy-start = (bf16[512,256]{1,0:T(8,128)(2,1)S(1)}, bf16[512,256]{1,0:T(8,128)(2,1)}, u32[]{:S(2)}) copy-start(bf16[512,256]{1,0:T(8,128)(2,1)} %param.5) | copy-start | bytes 786436
  11.2 85.9 %collective-permute-start = (bf16[16,256,256]{2,1,0:T(8,128)(2,1)}, bf16[16,256,256]{2,1,0:T(8,128)(2,1)}, u32[]{:S(2)}, u32[]{:S(2)}) collective-permute-start(bf16[16,256,256]{2,1,0:T(8,128)(2,1)} %bitcast.18), channel_id=1, source_target_pairs={{0,1},{1,0},{2,3},{3,2},{4,5},{5,4},{6,7},{7,6},{8,9},{9,8},{10,11... | collective-permute-start | bytes 6291464 | tf_op jit(solution)/shard_map/ppermute | solution.py:58
  22.1 27.5 %all-to-all-start = ((bf16[32,8,256]{2,1,0:T(8,128)(2,1)}), bf16[32,8,256]{2,1,0:T(8,128)(2,1)S(1)}, u32[]{:S(2)}, u32[]{:S(2)}) async-start(bf16[32,8,256]{2,1,0:T(8,128)(2,1)} %copy.21), calls=%async_computation | async-start | bytes 262144 | tf_op jit(solution)/shard_map/all_to_all | solution.py:43
  97.1 6.4 %copy-start.2 = (bf16[8192,256]{1,0:T(8,128)(2,1)S(1)}, bf16[8192,256]{1,0:T(8,128)(2,1)}, u32[]{:S(2)}) copy-start(bf16[8192,256]{1,0:T(8,128)(2,1)} %all-gather.6.cloned.1.call-done) | copy-start | bytes 12582916
  101.3 3.8 %collective-permute-start.1 = (f32[512,256]{1,0:T(8,128)S(1)}, f32[512,256]{1,0:T(8,128)S(1)}, u32[]{:S(2)}, u32[]{:S(2)}) collective-permute-start(f32[512,256]{1,0:T(8,128)S(1)} %convolution_bitcast_fusion), channel_id=1, source_target_pairs={{0,1},{1,0},{2,3},{3,2},{4,5},{5,4},{6,7},{7,6},{8,9},{9,8},{10,11... | collective-permute-start | bytes 1572872 | tf_op jit(solution)/shard_map/ppermute | solution.py:89
Sparse Core Ops, SparseCore 0:
  9.4 85.2 all-gather.5
